TPU v7x, 32 devices: a whole 2x2x4 slice. The times are simulated.
32 devices in a mesh: row: 4 (over y, x), col: 8 (over z, core).
Axes of the slice: x: 2, y: 2, z: 4, core: 2. Of those that a mesh axis runs over, the one named last changes fastest.
Arguments:
- points: bfloat16 [8192, 256], P(('row', 'col')), may hold values from -0.4 to 0.4, as said below
- spread: float32 [8192], P(('row', 'col')), may hold values from 1 to 12
- vectors: bfloat16 [8192, 64], P(('row', 'col')), may hold values from -6 to 6
Outputs:
- product: float32 [8192, 64], P(('row', 'col'))
Inputs may be any that keep to these rules, and one draw needn't show every extreme that they name: `points`: embedding entries are real values of order 0.1.
All inputs are finite; a program needn't handle non-finite values.
Results may differ from a plain program's by a relative error of at most 0.0085.
Values may be sent and summed in bfloat16 or wider, within the bound.
A program may use at most 128 MiB of HBM per device.

v0:
```python
import jax
import jax.numpy as jnp
from jax import lax
from jax.sharding import PartitionSpec as P


def distances(left_pts, right_pts):
    left_f = left_pts.astype(jnp.float32)
    right_f = right_pts.astype(jnp.float32)
    left_sq = jnp.sum(left_f * left_f, axis=1)
    right_sq = jnp.sum(right_f * right_f, axis=1)
    cross = lax.dot_general(
        left_pts, right_pts, (((1,), (1,)), ((), ())), preferred_element_type=jnp.float32
    )
    return left_sq[:, None] + right_sq[None, :] - 2.0 * cross


def local(points, spread, vectors):
    share_rows = points.shape[0]
    n_rows = lax.axis_size("row")
    n_cols = lax.axis_size("col")
    row_pos = lax.axis_index("row")
    col_pos = lax.axis_index("col")
    blk_pts, blk_bw, blk_vec = (
        lax.all_gather(points, "col", axis=0, tiled=True),
        lax.all_gather(spread.astype(jnp.bfloat16), "col", axis=0, tiled=True).astype(spread.dtype),
        lax.all_gather(vectors, "col", axis=0, tiled=True),
    )
    crs_pts, crs_bw, crs_vec = (
        lax.all_gather(points, "row", axis=0, tiled=True),
        lax.all_gather(spread.astype(jnp.bfloat16), "row", axis=0, tiled=True).astype(spread.dtype),
        lax.all_gather(vectors, "row", axis=0, tiled=True),
    )
    blk_local = jnp.arange(share_rows * n_cols, dtype=jnp.int32)
    blk_ids = row_pos * (n_cols * share_rows) + blk_local
    crs_local = jnp.arange(share_rows * n_rows, dtype=jnp.int32)
    crs_ids = (
        crs_local // share_rows * (n_cols * share_rows)
        + col_pos * share_rows
        + crs_local % share_rows
    )
    same = blk_ids[:, None] == crs_ids[None, :]
    dist = distances(blk_pts, crs_pts)
    kernel = jnp.where(same, jnp.float32(0.0), jnp.exp(-blk_bw[:, None] * dist))
    totals = lax.psum(jnp.sum(kernel, axis=1), "col")
    norm = (kernel / totals[:, None]).astype(jnp.bfloat16)
    to_cross = lax.dot_general(
        norm, blk_vec, (((0,), (0,)), ((), ())), preferred_element_type=jnp.float32
    )
    mirror = jnp.where(same, jnp.float32(0.0), jnp.exp(-crs_bw[None, :] * dist))
    mirror_tot = lax.psum(jnp.sum(mirror, axis=0), "row")
    mirror_norm = (mirror / mirror_tot[None, :]).astype(jnp.bfloat16)
    to_cross = to_cross + lax.dot_general(
        mirror_norm, blk_vec, (((0,), (0,)), ((), ())), preferred_element_type=jnp.float32
    )
    summed = lax.psum_scatter(to_cross, "row", scatter_dimension=0, tiled=True)
    return 0.5 * summed


def solution(mesh):
    placed = (P(("row", "col"), None), P(("row", "col")), P(("row", "col"), None))
    return jax.shard_map(
        local, mesh=mesh, in_specs=placed, out_specs=P(("row", "col"), None), check_vma=False
    )
```

profile of v0, /device:TPU:0, one launch (start us, length us, event | category | flops | bytes accessed | tf_op | source)
XLA Modules:
  0.0 126.9 jit_solution(6512187139585747209)
XLA Ops:
  6.5 0.0 all-gather.4.cloned.1.call-start
  6.5 0.7 all-gather.4.cloned.1.call-update
  7.3 0.0 reduce-scatter.2.cloned.1.call-start
  7.3 0.7 convert_element_type.22
  8.0 9.5 %all-gather.1 = bf16[4,1,256]{2,1,0:T(2,128)(2,1)S(1)} all-gather(bf16[1,1,256]{2,1,0:T(2,128)(2,1)S(1)} %reshape.35), channel_id=1, replica_groups=mesh['row'=4,'col'=8] {'row'}, dimensions={0}, use_global_device_ids=true | all-gather | bytes 2560 | tf_op jit(solution)/shard_map/all_gather | solution.py:31
  17.5 12.0 %all-gather = bf16[8,1,256]{2,1,0:T(2,128)(2,1)S(1)} all-gather(bf16[1,1,256]{2,1,0:T(2,128)(2,1)S(1)} %reshape.35), channel_id=1, replica_groups=mesh['row'=4,'col'=8] {'col'}, dimensions={0}, use_global_device_ids=true | all-gather | bytes 4608 | tf_op jit(solution)/shard_map/all_gather | solution.py:26
  29.5 10.3 %all_gather.17 = bf16[1024,256]{1,0:T(8,128)(2,1)S(1)} all-gather(bf16[256,256]{1,0:T(8,128)(2,1)} %param.3), channel_id=1, replica_groups=mesh['row'=4,'col'=8] {'row'}, dimensions={0}, use_global_device_ids=true | all-gather | bytes 655360 | tf_op jit(solution)/shard_map/all_gather | solution.py:30
  39.8 14.4 %all_gather.18 = bf16[2048,64]{0,1:T(8,128)(2,1)S(1)} all-gather(bf16[256,64]{0,1:T(8,128)(2,1)} %param.5), channel_id=1, replica_groups=mesh['row'=4,'col'=8] {'col'}, dimensions={0}, use_global_device_ids=true | all-gather | bytes 294912 | tf_op jit(solution)/shard_map/all_gather | solution.py:27
  54.2 0.2 multiply_reduce_fusion.1
  54.5 0.0 all-gather.4.cloned.1.call-done
  54.5 1.6 %multiply_reduce_fusion = f32[2048]{0:T(1024)S(1)} fusion(bf16[2048,256]{1,0:T(8,128)(2,1)} %all-gather.4.cloned.1.call-done), kind=kLoop, calls=%fused_computation.9 | loop fusion | flops 1570816 | bytes 1056768 | tf_op jit(solution)/shard_map/reduce_sum | solution.py:10
  56.1 7.5 %fusion = (f32[2048]{0:T(1024)S(1)}, f32[1024]{0:T(1024)S(1)}, f32[2048,1024]{1,0:T(8,128)}) fusion(f32[1024]{0:T(1024)S(1)} %multiply_reduce_fusion.1, f32[2048]{0:T(1024)S(1)} %multiply_reduce_fusion, f32[2048]{0:T(1024)S(1)} %bitcast.6, s32[1024]{0:T(1024)S(1)} %fusion.13, s32[2048]{0:T(1024)S(1)} %iota_add_fusion, f32[1024]{0:T(1024)S(1)} %bitcast.8, ...), kind=kOutput, calls=%fused_computation.5 | convolution fusion | flops 1094710272 | bytes 10010624 | tf_op jit(solution)/shard_map/dot_general | solution.py:12
  63.6 8.9 %psum.15 = f32[1024]{0:T(1024)S(1)} all-reduce(f32[1024]{0:T(1024)S(1)} %get-tuple-element.6), channel_id=1, replica_groups=mesh['row'=4,'col'=8] {'row'}, use_global_device_ids=true, to_apply=%region_5.6 | all-reduce | flops 1024 | bytes 8192 | tf_op jit(solution)/shard_map/psum | solution.py:51
  72.5 13.9 %psum.14 = f32[2048]{0:T(1024)S(1)} all-reduce(f32[2048]{0:T(1024)S(1)} %get-tuple-element.5), channel_id=1, replica_groups=mesh['row'=4,'col'=8] {'col'}, use_global_device_ids=true, to_apply=%region_3.4 | all-reduce | flops 2048 | bytes 16384 | tf_op jit(solution)/shard_map/psum | solution.py:45
  86.4 0.0 copy-start
  86.4 6.9 %fusion.2 = f32[1024,64]{0,1:T(8,128)S(1)} fusion(bf16[2048,64]{0,1:T(8,128)(2,1)S(1)} %all_gather.18, f32[2048,1024]{1,0:T(8,128)} %get-tuple-element.7, f32[1024]{0:T(1024)S(1)} %psum.15, f32[1024]{0:T(1024)S(1)} %bitcast.9, f32[1024]{0:T(1024)S(1)} %multiply_reduce_fusion.1, f32[2048]{0:T(1024)S(1)} %multiply_reduce_fusion, s32[1024]{0:T(1024)S(1)} %fusion.13, ...), kind=kOutput, calls=%fused_computation.7 | convolution fusion | flops 285212672 | bytes 8945664 | tf_op jit(solution)/shard_map/dot_general | solution.py:53
  93.3 0.0 copy-done
  93.3 3.8 %fusion.4 = f32[1024,64]{0,1:T(8,128)} fusion(f32[1024,64]{0,1:T(8,128)S(1)} %fusion.2, bf16[2048,64]{0,1:T(8,128)(2,1)S(1)} %all_gather.18, f32[2048,1024]{1,0:T(8,128)S(1)} %copy-done, f32[2048]{0:T(1024)S(1)} %psum.14, f32[1024]{0:T(1024)S(1)} %multiply_reduce_fusion.1, f32[2048]{0:T(1024)S(1)} %multiply_reduce_fusion, f32[2048]{0:T(1024)S(1)} %bitcast.7, ...), kind=kOutput, calls=%fused_computation.10 | convolution fusion | flops 285278208 | bytes 9216000 | tf_op jit(solution)/shard_map/dot_general | solution.py:47
  97.1 0.0 reduce-scatter.2.cloned.1.call-update
  97.2 21.5 %reduce-scatter.2.cloned.1.call-done = f32[256,64]{0,1:T(8,128)} async-done(((f32[1024,64]{0,1:T(8,128)}), f32[256,64]{0,1:T(8,128)}) %reduce-scatter.2.cloned.1.call-update) | async-done | bytes 65552 | tf_op jit(solution)/shard_map/reduce_scatter | solution.py:56
  118.6 1.5 %broadcast_multiply_fusion = f32[256,64]{0,1:T(8,128)} fusion(f32[256,64]{0,1:T(8,128)} %reduce-scatter.2.cloned.1.call-done), kind=kLoop, calls=%fused_computation.12 | loop fusion | flops 16384 | bytes 131072 | tf_op jit(solution)/shard_map/mul | solution.py:57
  (5 shorter events, 0.0 us)
Async XLA Ops:
  6.5 47.9 %all-gather.4.cloned.1.call-start = ((), (), s32[]{:S(2)}) async-start(), calls=%async_computation.1 | async-start | bytes 1179648 | tf_op jit(solution)/shard_map/all_gather | solution.py:25
  7.3 111.4 %reduce-scatter.2.cloned.1.call-start = ((), (), s32[]{:S(2)}) async-start(), calls=%async_computation.2 | async-start | bytes 327680 | tf_op jit(solution)/shard_map/reduce_scatter | solution.py:56
  86.4 6.9 %copy-start = (f32[2048,1024]{1,0:T(8,128)S(1)}, f32[2048,1024]{1,0:T(8,128)}, u32[]{:S(2)}) copy-start(f32[2048,1024]{1,0:T(8,128)} %get-tuple-element.7) | copy-start | bytes 25165828
Sparse Core Ops, SparseCore 0:
  9.0 24.7 all-gather.3
  97.3 21.3 reduce-scatter.1
where the time goes:
time: 127 us
  blocking collectives  69 us (54%)
  waiting for transfers between devices  22.2 us (17%)
  matrix products  18.2 us (14%)
  between operations  13.5 us (11%)
  other arithmetic  3.97 us (3%)
    reduce_scatter x1, waiting for transfers between devices, local(): summed = lax.psum_scatter(to_cross, 'row', scatter_dimension=0, tiled=True)  21.5 us
    all_gather x1, blocking collectives, local(): lax.all_gather(vectors, 'col', axis=0, tiled=True)  14.4 us
    psum x1, blocking collectives, local(): totals = lax.psum(jnp.sum(kernel, axis=1), 'col')  13.9 us
    all_gather x1, blocking collectives, local(): lax.all_gather(spread.astype(jnp.bfloat16), 'col', axis=0, tiled=True)  12 us
    all_gather x1, blocking collectives, local(): lax.all_gather(points, 'row', axis=0, tiled=True)  10.3 us
    all_gather x1, blocking collectives, local(): lax.all_gather(spread.astype(jnp.bfloat16), 'row', axis=0, tiled=True)  9.5 us
    psum x1, blocking collectives, local(): mirror_tot = lax.psum(jnp.sum(mirror, axis=0), 'row')  8.9 us
    dot_general x1, matrix products, distances(): lax.dot_general(left_pts, right_pts, (((1,), (1,)), ((), ())), preferred_...  7.5 us
  transfers between devices with their start and end apart: 2, of which 1 were waited for; matrix products, arithmetic and copies ran while one was open for 1% of the time, Pallas kernels for 0%

commit v1 on v0

--- a/solution.py
+++ b/solution.py
@@ -2,6 +2,18 @@
 import jax.numpy as jnp
 from jax import lax
 from jax.sharding import PartitionSpec as P
+
+
+def doubled_up(x, axis, dim):
+    ways, here = (lax.axis_size(axis), lax.axis_index(axis))
+    grown, reach = (x, 1)
+    while reach < ways:
+        theirs = lax.ppermute(grown, axis, [(d, d ^ reach) for d in range(ways)])
+        mine_first = jnp.concatenate([grown, theirs], axis=dim)
+        theirs_first = jnp.concatenate([theirs, grown], axis=dim)
+        grown = jnp.where(here & reach == 0, mine_first, theirs_first)
+        reach = 2 * reach
+    return grown
 
 
 def distances(left_pts, right_pts):
@@ -28,7 +40,7 @@
     )
     crs_pts, crs_bw, crs_vec = (
         lax.all_gather(points, "row", axis=0, tiled=True),
-        lax.all_gather(spread.astype(jnp.bfloat16), "row", axis=0, tiled=True).astype(spread.dtype),
+        doubled_up(spread.astype(jnp.bfloat16), "row", 0).astype(spread.dtype),
         lax.all_gather(vectors, "row", axis=0, tiled=True),
     )
     blk_local = jnp.arange(share_rows * n_cols, dtype=jnp.int32)

time: 127 us -> 124 us (0.976)
  blocking collectives: 69 us -> 59.6 us
  starting transfers between devices: 0.04 us -> 4.52 us
  waiting for transfers between devices: 22.2 us -> 24.3 us
    all_gather x1 -> x0, blocking collectives: 9.5 us -> none  [local(): lax.all_gather(spread.astype(jnp.bfloat16), 'row', axis=0, tiled=True)]
    ppermute x0 -> x2, starting transfers between devices: none -> 4.48 us  [doubled_up(): theirs = lax.ppermute(grown, axis, [(d, d ^ reach) for d in range(ways)])]
    ppermute x0 -> x2, waiting for transfers between devices: none -> 2.09 us  [doubled_up(): theirs = lax.ppermute(grown, axis, [(d, d ^ reach) for d in range(ways)])]
  transfers between devices with their start and end apart: 2 -> 4, of which waited for: 1 -> 2; matrix products, arithmetic and copies ran while one was open for 1% -> 1% of each run, Pallas kernels for 0% -> 0%
where the time goes in v1:
time: 124 us
  blocking collectives  59.6 us (48%)
  waiting for transfers between devices  24.3 us (20%)
  matrix products  18.2 us (15%)
  between operations  13.5 us (11%)
  starting transfers between devices  4.52 us (4%)
  other arithmetic  3.98 us (3%)
    reduce_scatter x1, waiting for transfers between devices, local(): summed = lax.psum_scatter(to_cross, 'row', scatter_dimension=0, tiled=True)  21.5 us
    all_gather x1, blocking collectives, local(): lax.all_gather(vectors, 'col', axis=0, tiled=True)  14.4 us
    psum x1, blocking collectives, local(): totals = lax.psum(jnp.sum(kernel, axis=1), 'col')  13.9 us
    all_gather x1, blocking collectives, local(): lax.all_gather(spread.astype(jnp.bfloat16), 'col', axis=0, tiled=True)  12 us
    all_gather x1, blocking collectives, local(): lax.all_gather(points, 'row', axis=0, tiled=True)  10.4 us
    psum x1, blocking collectives, local(): mirror_tot = lax.psum(jnp.sum(mirror, axis=0), 'row')  8.91 us
    dot_general x1, matrix products, distances(): lax.dot_general(left_pts, right_pts, (((1,), (1,)), ((), ())), preferred_...  7.47 us
    dot_general x1, matrix products, local(): lax.dot_general(mirror_norm, blk_vec, (((0,), (0,)), ((), ())), preferred...  6.88 us
  transfers between devices with their start and end apart: 4, of which 2 were waited for; matrix products, arithmetic and copies ran while one was open for 1% of the time, Pallas kernels for 0%

profile of v1, /device:TPU:0, one launch (start us, length us, event | category | flops | bytes accessed | tf_op | source)
XLA Modules:
  0.0 124.1 jit_solution(7497700386192561572)
XLA Ops:
  6.5 0.0 all-gather.3.cloned.1.call-start
  6.5 0.7 all-gather.3.cloned.1.call-update
  7.3 0.0 reduce-scatter.2.cloned.1.call-start
  7.3 0.7 convert_element_type.26
  8.0 2.9 %collective-permute-start = (bf16[256]{0:T(256)(128)(2,1)S(1)}, bf16[256]{0:T(256)(128)(2,1)S(1)}, u32[]{:S(2)}, u32[]{:S(2)}) collective-permute-start(bf16[256]{0:T(256)(128)(2,1)S(1)} %convert_element_type.26), channel_id=1, source_target_pairs={{0,8},{8,0},{16,24},{24,16},{1,9},{9,1},{17,25},{25,17},{2,10},{10... | collective-permute-start | bytes 1544 | tf_op jit(solution)/shard_map/ppermute | solution.py:11
  10.9 12.0 %all-gather = bf16[8,1,256]{2,1,0:T(2,128)(2,1)S(1)} all-gather(bf16[1,1,256]{2,1,0:T(2,128)(2,1)S(1)} %reshape.81), channel_id=1, replica_groups=mesh['row'=4,'col'=8] {'col'}, dimensions={0}, use_global_device_ids=true | all-gather | bytes 4608 | tf_op jit(solution)/shard_map/all_gather | solution.py:38
  22.9 10.4 %all_gather.14 = bf16[1024,256]{1,0:T(8,128)(2,1)S(1)} all-gather(bf16[256,256]{1,0:T(8,128)(2,1)} %param.3), channel_id=1, replica_groups=mesh['row'=4,'col'=8] {'row'}, dimensions={0}, use_global_device_ids=true | all-gather | bytes 655360 | tf_op jit(solution)/shard_map/all_gather | solution.py:42
  33.3 14.4 %all_gather.15 = bf16[2048,64]{0,1:T(8,128)(2,1)S(1)} all-gather(bf16[256,64]{0,1:T(8,128)(2,1)} %param.5), channel_id=1, replica_groups=mesh['row'=4,'col'=8] {'col'}, dimensions={0}, use_global_device_ids=true | all-gather | bytes 294912 | tf_op jit(solution)/shard_map/all_gather | solution.py:39
  47.7 0.2 multiply_reduce_fusion.1
  48.0 0.0 collective-permute-done
  48.0 1.5 %collective-permute-start.1 = (bf16[512]{0:T(512)(128)(2,1)S(1)}, bf16[512]{0:T(512)(128)(2,1)S(1)}, u32[]{:S(2)}, u32[]{:S(2)}) collective-permute-start(bf16[512]{0:T(512)(128)(2,1)S(1)} %maximum_select_fusion.1), channel_id=1, source_target_pairs={{0,16},{8,24},{16,0},{24,8},{1,17},{9,25},{17,1},{25,9},{2,18},{10... | collective-permute-start | bytes 3080 | tf_op jit(solution)/shard_map/ppermute | solution.py:11
  49.6 2.1 %collective-permute-done.1 = bf16[512]{0:T(512)(128)(2,1)S(1)} collective-permute-done((bf16[512]{0:T(512)(128)(2,1)S(1)}, bf16[512]{0:T(512)(128)(2,1)S(1)}, u32[]{:S(2)}, u32[]{:S(2)}) %collective-permute-start.1) | collective-permute-done | bytes 1056 | tf_op jit(solution)/shard_map/ppermute | solution.py:11
  51.7 0.0 all-gather.3.cloned.1.call-done
  51.7 1.6 %multiply_reduce_fusion = f32[2048]{0:T(1024)S(1)} fusion(bf16[2048,256]{1,0:T(8,128)(2,1)} %all-gather.3.cloned.1.call-done), kind=kLoop, calls=%fused_computation.9 | loop fusion | flops 1570816 | bytes 1056768 | tf_op jit(solution)/shard_map/reduce_sum | solution.py:22
  53.3 7.5 %fusion = (f32[2048]{0:T(1024)S(1)}, f32[1024]{0:T(1024)S(1)}, f32[2048,1024]{1,0:T(8,128)}) fusion(f32[1024]{0:T(1024)S(1)} %multiply_reduce_fusion.1, f32[2048]{0:T(1024)S(1)} %multiply_reduce_fusion, f32[2048]{0:T(1024)S(1)} %bitcast.5, s32[1024]{0:T(1024)S(1)} %fusion.13, s32[2048]{0:T(1024)S(1)} %iota_add_fusion, f32[1024]{0:T(1024)S(1)} %convert_negate_fusion.1, ...), kind=kOutput, calls=%fused_computation.5 | convolution fusion | flops 1094710272 | bytes 10010624 | tf_op jit(solution)/shard_map/dot_general | solution.py:24
  60.7 8.9 %psum.15 = f32[1024]{0:T(1024)S(1)} all-reduce(f32[1024]{0:T(1024)S(1)} %get-tuple-element.6), channel_id=1, replica_groups=mesh['row'=4,'col'=8] {'row'}, use_global_device_ids=true, to_apply=%region_5.6 | all-reduce | flops 1024 | bytes 8192 | tf_op jit(solution)/shard_map/psum | solution.py:63
  69.6 13.9 %psum.14 = f32[2048]{0:T(1024)S(1)} all-reduce(f32[2048]{0:T(1024)S(1)} %get-tuple-element.5), channel_id=1, replica_groups=mesh['row'=4,'col'=8] {'col'}, use_global_device_ids=true, to_apply=%region_3.4 | all-reduce | flops 2048 | bytes 16384 | tf_op jit(solution)/shard_map/psum | solution.py:57
  83.5 0.0 copy-start
  83.6 6.9 %fusion.2 = f32[1024,64]{0,1:T(8,128)S(1)} fusion(bf16[2048,64]{0,1:T(8,128)(2,1)S(1)} %all_gather.15, f32[2048,1024]{1,0:T(8,128)} %get-tuple-element.7, f32[1024]{0:T(1024)S(1)} %psum.15, f32[1024]{0:T(1024)S(1)} %convert_negate_fusion.1, f32[1024]{0:T(1024)S(1)} %multiply_reduce_fusion.1, f32[2048]{0:T(1024)S(1)} %multiply_reduce_fusion, ...), kind=kOutput, calls=%fused_computation.7 | convolution fusion | flops 285212672 | bytes 8945664 | tf_op jit(solution)/shard_map/dot_general | solution.py:65
  90.4 0.0 copy-done
  90.5 3.8 %fusion.4 = f32[1024,64]{0,1:T(8,128)} fusion(f32[1024,64]{0,1:T(8,128)S(1)} %fusion.2, bf16[2048,64]{0,1:T(8,128)(2,1)S(1)} %all_gather.15, f32[2048,1024]{1,0:T(8,128)S(1)} %copy-done, f32[2048]{0:T(1024)S(1)} %psum.14, f32[1024]{0:T(1024)S(1)} %multiply_reduce_fusion.1, f32[2048]{0:T(1024)S(1)} %multiply_reduce_fusion, f32[2048]{0:T(1024)S(1)} %bitcast.6, ...), kind=kOutput, calls=%fused_computation.10 | convolution fusion | flops 285278208 | bytes 9216000 | tf_op jit(solution)/shard_map/dot_general | solution.py:59
  94.3 0.0 reduce-scatter.2.cloned.1.call-update
  94.3 21.5 %reduce-scatter.2.cloned.1.call-done = f32[256,64]{0,1:T(8,128)} async-done(((f32[1024,64]{0,1:T(8,128)}), f32[256,64]{0,1:T(8,128)}) %reduce-scatter.2.cloned.1.call-update) | async-done | bytes 65552 | tf_op jit(solution)/shard_map/reduce_scatter | solution.py:68
  115.8 1.5 %broadcast_multiply_fusion = f32[256,64]{0,1:T(8,128)} fusion(f32[256,64]{0,1:T(8,128)} %reduce-scatter.2.cloned.1.call-done), kind=kLoop, calls=%fused_computation.12 | loop fusion | flops 16384 | bytes 131072 | tf_op jit(solution)/shard_map/mul | solution.py:69
  (6 shorter events, 0.0 us)
Async XLA Ops:
  6.5 45.1 %all-gather.3.cloned.1.call-start = ((), (), s32[]{:S(2)}) async-start(), calls=%async_computation.1 | async-start | bytes 1179648 | tf_op jit(solution)/shard_map/all_gather | solution.py:37
  7.3 108.5 %reduce-scatter.2.cloned.1.call-start = ((), (), s32[]{:S(2)}) async-start(), calls=%async_computation.2 | async-start | bytes 327680 | tf_op jit(solution)/shard_map/reduce_scatter | solution.py:68
  8.0 40.0 %collective-permute-start = (bf16[256]{0:T(256)(128)(2,1)S(1)}, bf16[256]{0:T(256)(128)(2,1)S(1)}, u32[]{:S(2)}, u32[]{:S(2)}) collective-permute-start(bf16[256]{0:T(256)(128)(2,1)S(1)} %convert_element_type.26), channel_id=1, source_target_pairs={{0,8},{8,0},{16,24},{24,16},{1,9},{9,1},{17,25},{25,17},{2,10},{10... | collective-permute-start | bytes 1544 | tf_op jit(solution)/shard_map/ppermute | solution.py:11
  48.0 3.6 %collective-permute-start.1 = (bf16[512]{0:T(512)(128)(2,1)S(1)}, bf16[512]{0:T(512)(128)(2,1)S(1)}, u32[]{:S(2)}, u32[]{:S(2)}) collective-permute-start(bf16[512]{0:T(512)(128)(2,1)S(1)} %maximum_select_fusion.1), channel_id=1, source_target_pairs={{0,16},{8,24},{16,0},{24,8},{1,17},{9,25},{17,1},{25,9},{2,18},{10... | collective-permute-start | bytes 3080 | tf_op jit(solution)/shard_map/ppermute | solution.py:11
  83.5 6.9 %copy-start = (f32[2048,1024]{1,0:T(8,128)S(1)}, f32[2048,1024]{1,0:T(8,128)}, u32[]{:S(2)}) copy-start(f32[2048,1024]{1,0:T(8,128)} %get-tuple-element.7) | copy-start | bytes 25165828
Sparse Core Ops, SparseCore 0:
  9.0 24.8 all-gather.2
  94.4 21.3 reduce-scatter.1
